TPU v7x, 256 devices: a whole 4x4x8 slice. The times are simulated.
256 devices in a mesh: src: 16 (over y, x), tgt: 16 (over z, core).
Axes of the slice: x: 4, y: 4, z: 8, core: 2. Of those that a mesh axis runs over, the one named last changes fastest.
Arguments:
- pcs_source: bfloat16 [30, 32768], P(None, 'src'), may hold values from -6 to 10
- pcs_target: bfloat16 [30, 32768], P(None, 'tgt'), may hold values from -6 to 6
- growth: float32 [32768], P('src'), may hold values from 0.25 to 4
- scores: bfloat16 [32768, 128], P('src'), may hold values from -6 to 6
Outputs:
- source_potential: float32 [32768], P('src')
- target_potential: float32 [32768], P('tgt')
- transported: float32 [32768, 128], P('tgt')
All inputs are finite; a program needn't handle non-finite values.
Results may differ from a plain program's by a relative error of at most 0.0029.
Values sent between devices are 32-bit elements; how exact they have to be, the bound alone decides.
No kernel may reach another device: no remote copies, remote signals or barrier semaphores. Data moves between devices by JAX's collectives and lax.ppermute only.
A program may use at most 64 MiB of HBM per device.

v0:
```python
import functools
import math

import jax
import jax.numpy as jnp
from jax import lax
from jax.experimental import pallas as pl
from jax.experimental.pallas import tpu as pltpu
from jax.sharding import PartitionSpec as P

ITERS = 2
EPSILON = 0.05
MARGIN = 1.0
FACTOR = MARGIN / (MARGIN + EPSILON)

UNIT = EPSILON * math.log(2.0)
LOW, HIGH, LEAST = 2.0**-90, 2.0**100, 2.0**-100
STATIC, DEPTH = 96, 112
TILE = 256
f32, bf16 = jnp.float32, jnp.bfloat16


def split3(v):
    high = v.astype(bf16).astype(f32)
    rest = v - high
    mid = rest.astype(bf16).astype(f32)
    return high, mid, (rest - mid).astype(bf16).astype(f32)


def rows_of(values, count):
    row = lax.broadcasted_iota(jnp.int32, (count, values[0].shape[-1]), 0)
    out = jnp.zeros(row.shape, f32)
    for k, v in enumerate(values):
        out = jnp.where(row == k, v, out)
    return out.astype(bf16)


def set_source(left, u):
    one = jnp.ones_like(u)
    left[STATIC:, :] = rows_of([*split3(u), one, one, one], DEPTH - STATIC)


def set_target(right, v):
    one = jnp.ones_like(v)
    right[STATIC:, :] = rows_of([one, one, one, *split3(v)], DEPTH - STATIC)


def tile_of(ref, k):
    return ref[:, pl.ds(pl.multiple_of(k * TILE, TILE), TILE)]


def logits(first, second):
    return lax.dot_general(first, second, (((0,), (0,)), ((), ())), preferred_element_type=f32)


def log_sum(first, second):
    count = first.shape[1] // TILE

    def peaks(k, peak):
        return jnp.maximum(peak, jnp.max(logits(tile_of(first, k), second[...]), axis=0, keepdims=True))

    peak = lax.fori_loop(0, count, peaks, jnp.full((1, second.shape[1]), -jnp.inf, f32))

    def totals(k, total):
        part = jnp.exp2(logits(tile_of(first, k), second[...]) - peak)
        return total + jnp.sum(part, axis=0, keepdims=True)

    total = lax.fori_loop(0, count, totals, jnp.zeros_like(peak))
    return peak, total


def merged(parts):
    peak = jnp.max(parts, axis=0)
    return peak + jnp.log2(jnp.sum(jnp.exp2(parts - peak[None]), axis=0))


def in_range(total, weight=None):
    fine = jnp.logical_and(jnp.min(total) >= LOW, jnp.max(total) <= HIGH)
    return fine if weight is None else jnp.logical_and(fine, jnp.min(weight) >= LEAST)


def send_copies(out, value):
    out[...] = jnp.broadcast_to(value[None], out.shape)


def first_rows(
    scale, xy_ref, out, left, right, asq, bsq, shift, kernel, across, turned
):
    xp = xy_ref[:32, :]
    xw = xp.astype(f32)
    y = xy_ref[32:, :].astype(f32)
    for k, part in enumerate(split3(y * (2.0 * scale))):
        left[32 * k : 32 * k + 32, :] = xp
        right[32 * k : 32 * k + 32, :] = part.astype(bf16)
    asq[...] = jnp.sum(xw * xw, axis=0, keepdims=True) * scale
    bsq[...] = jnp.sum(y * y, axis=0, keepdims=True) * scale
    set_source(left, -asq[...])
    set_target(right, -bsq[...])
    turned[...] = jnp.transpose(right[...])
    size = xp.shape[1]
    chunk = 512
    for n in range(0, size, chunk):
        part = jnp.dot(turned[:TILE, :], left[:, n : n + chunk], preferred_element_type=f32)
        shift[:, n : n + chunk] = jnp.max(part, axis=0, keepdims=True)
    set_source(left, -asq[...] - shift[...])
    sums = []
    for n in range(0, size, chunk):
        total = jnp.zeros((8, chunk), f32)
        for k in range(0, size, TILE):
            part = jnp.dot(turned[k : k + TILE, :], left[:, n : n + chunk], preferred_element_type=f32)
            part = jnp.exp2(part)
            low = part.astype(bf16)
            across[k : k + TILE, n : n + chunk] = low
            kernel[n : n + chunk, k : k + TILE] = jnp.transpose(low)
            total = total + jnp.sum(part.reshape(TILE // 8, 8, chunk), axis=0)
        sums.append(jnp.sum(total, axis=0, keepdims=True))
    total = jnp.concatenate(sums, axis=1)
    out[...] = shift[...] + jnp.log2(total)

    @pl.when(jnp.logical_not(in_range(total)))
    def _():
        set_source(left, -asq[...])
        peak, exact = log_sum(right, left)
        out[...] = peak + jnp.log2(exact)


def source_weights(log_total, parts, growth, shift):
    rows = merged(parts[...])
    potential = FACTOR * (jnp.log2(growth[...]) - log_total - rows)
    log_weight = potential + shift[...]
    top = jnp.max(log_weight)
    return potential, jnp.exp2(log_weight - top), top


def weighted(lines, kernel):
    return jnp.dot(lines, kernel[...], preferred_element_type=f32)


def over_first(weight, kernel):
    return jnp.sum(weighted(rows_of(split3(weight), 16), kernel)[:3], axis=0, keepdims=True)


def columns(log_total, parts, growth, scores, shift, kernel, left0, right0, asq, bsq, out, sT, left, right):
    sT[...] = jnp.transpose(scores[...])
    potential, weight, top = source_weights(log_total, parts, growth, shift)
    total = over_first(weight, kernel)
    send_copies(out, top + jnp.log2(total))

    @pl.when(jnp.logical_not(in_range(total, weight)))
    def _():
        left[...] = left0[...]
        right[...] = right0[...]
        set_source(left, potential - asq[...])
        peak, exact = log_sum(left, right)
        send_copies(out, peak + jnp.log2(exact))


def rows(log_total, parts, shift, across, left0, right0, asq, bsq, out, left, right):
    potential = FACTOR * (-log_total - merged(parts[...]))
    top = jnp.max(potential)
    weight = jnp.exp2(potential - top)
    total = over_first(weight, across)
    out[...] = shift[...] + top + jnp.log2(total)

    @pl.when(jnp.logical_not(in_range(total, weight)))
    def _():
        left[...] = left0[...]
        right[...] = right0[...]
        set_source(left, -asq[...])
        set_target(right, potential - bsq[...])
        peak, exact = log_sum(right, left)
        out[...] = peak + jnp.log2(exact)


def pair(own, other, out):
    peak = jnp.maximum(own[...], other[...])
    total = jnp.exp2(own[...] - peak) + jnp.exp2(other[...] - peak)
    send_copies(out, peak + jnp.log2(total))


def put_blocks(out, carried, logs):
    count, lanes = out.shape[0], out.shape[2]
    progs = carried.shape[0]
    lines = jnp.concatenate([logs[:, d * lanes : (d + 1) * lanes] for d in range(count)], axis=0)
    for d in range(count):
        out[d, :progs, :] = carried[:, d * lanes : (d + 1) * lanes]
        out[d, progs:, :] = lines


def carry(log_total, parts, growth, shift, kernel, sT, left0, right0, asq, fout, out, left, right):
    potential, weight, top = source_weights(log_total, parts, growth, shift)
    fout[...] = potential * UNIT
    progs = sT.shape[0]
    scaled = sT[...].astype(f32) * weight
    high = scaled.astype(bf16)
    low = (scaled - high.astype(f32)).astype(bf16)
    sums = weighted(jnp.concatenate([high, low, rows_of(split3(weight), 16)], axis=0), kernel)
    total = jnp.sum(sums[2 * progs : 2 * progs + 3], axis=0, keepdims=True)
    put_blocks(out, (sums[:progs] + sums[progs : 2 * progs]) / total, top + jnp.log2(total))

    @pl.when(jnp.logical_not(in_range(total, weight)))
    def _():
        left[...] = left0[...]
        right[...] = right0[...]
        set_source(left, potential - asq[...])
        peak, exact = log_sum(left, right)

        def step(k, sums):
            plan = jnp.exp2(logits(tile_of(left, k), right[...]) - peak).astype(bf16)
            return sums + jnp.dot(tile_of(sT, k), plan, preferred_element_type=f32)

        start = jnp.zeros((progs, right.shape[1]), f32)
        sums = lax.fori_loop(0, left.shape[1] // TILE, step, start)
        put_blocks(out, sums / exact, peak + jnp.log2(exact))


def finish(log_total, parts, g, out):
    count, lanes = parts.shape[0], parts.shape[2]
    progs = parts.shape[1] - count
    g[...] = FACTOR * (-log_total - merged(parts[:, progs:, :])) * UNIT
    me = place_in_skewed(count)
    logs = [parts[d, pl.ds(progs + me, 1), :] for d in range(count)]
    peak = functools.reduce(jnp.maximum, logs)
    weights = [jnp.exp2(line - peak) for line in logs]
    total = sum(weights)
    carried = jnp.zeros((progs, lanes), f32)
    for d in range(count):
        carried = carried + (weights[d] / total) * parts[d, :progs, :]
    out[...] = jnp.broadcast_to(jnp.transpose(carried)[None], out.shape)


VMEM = pl.BlockSpec(memory_space=pltpu.VMEM)


def call(kernel, outs, specs, scratch=(), flops=10**7, name=None):
    return pl.pallas_call(
        kernel,
        out_shape=outs,
        in_specs=specs,
        scratch_shapes=list(scratch),
        compiler_params=pltpu.CompilerParams(vmem_limit_bytes=24 << 20),
        cost_estimate=pl.CostEstimate(flops=flops, bytes_accessed=1 << 20, transcendentals=0),
        name=name,
    )


def exchanged(x, axis, groups=None):
    return lax.all_to_all(x, axis, 0, 0, tiled=True, axis_index_groups=groups)


def rows_exchanged(line, targets):
    other = lax.ppermute(line, "tgt", [(k, k ^ 1) for k in range(targets)])
    copies = jax.ShapeDtypeStruct((targets // 2, *line.shape), f32)
    merged_line = call(pair, copies, [VMEM] * 2, name="pair")(line, other)
    chips = [[2 * z + core for z in range(targets // 2)] for core in range(2)]
    return exchanged(merged_line, "tgt", chips)


def skewed(sources):
    side = math.isqrt(sources)
    return [[(p // side) * side + (p + p // side) % side for p in range(sources)]]


def place_in_skewed(sources):
    side = math.isqrt(sources)
    me = lax.axis_index("src")
    y, x = me // side, me % side
    return y * side + (x - y + side) % side


def shards(pcs_source, pcs_target, growth, scores):
    count, size = pcs_source.shape
    progs = scores.shape[1]
    sources, targets = lax.axis_size("src"), lax.axis_size("tgt")
    own = size // sources
    log_sources = math.log2(size * sources)
    log_targets = math.log2(pcs_target.shape[1] * targets)
    scale = math.log2(math.e) / (EPSILON * count)
    shape = jax.ShapeDtypeStruct
    line = shape((1, size), f32)
    square = shape((size, size), bf16)
    operand = shape((DEPTH, size), bf16)
    operands = [pltpu.VMEM((DEPTH, size), bf16), pltpu.VMEM((DEPTH, size), bf16)]
    to_sources = shape((sources, 1, size), f32)

    pad = jnp.zeros((32 - count, size), bf16)
    local, left, right, asq, bsq, shift, kernel, across = call(
        functools.partial(first_rows, scale),
        (line, operand, operand, line, line, line, square, square),
        [VMEM],
        [pltpu.VMEM((size, DEPTH), bf16)],
        flops=4 * 10**9,
        name="first_rows",
    )(jnp.concatenate([pcs_source, pad, pcs_target, pad]))
    growth = growth.reshape(1, size)
    parts = rows_exchanged(local, targets)
    for _ in range(ITERS - 1):
        local, sT = call(
            functools.partial(columns, log_sources),
            (to_sources, shape((progs, size), bf16)),
            [VMEM] * 9,
            operands,
            name="columns",
        )(parts, growth, scores, shift, kernel, left, right, asq, bsq)
        parts = exchanged(local, "src", skewed(sources))
        local = call(functools.partial(rows, log_targets), line, [VMEM] * 7, operands, name="rows")(
            parts, shift, across, left, right, asq, bsq
        )
        parts = rows_exchanged(local, targets)
    potential, blocks = call(
        functools.partial(carry, log_sources),
        (line, shape((sources, progs + sources, own), f32)),
        [VMEM] * 8,
        operands,
        name="carry",
    )(parts, growth, shift, kernel, sT, left, right, asq)
    blocks = exchanged(blocks, "src", skewed(sources))
    g, result = call(
        functools.partial(finish, log_targets),
        (shape((sources, own), f32), shape((sources, own, progs), f32)),
        [VMEM],
        name="finish",
    )(blocks)
    transported = exchanged(result, "src", skewed(sources))
    return potential.reshape(size), g.reshape(size), transported.reshape(size, progs)


def solution(mesh):
    in_specs = (P(None, "src"), P(None, "tgt"), P("src"), P("src", None))
    out_specs = (P("src"), P("tgt"), P("tgt", None))
    return jax.shard_map(shards, mesh=mesh, in_specs=in_specs, out_specs=out_specs, check_vma=False)
```

profile of v0, /device:TPU:8, one launch (start us, length us, event | category | flops | bytes accessed | tf_op | source)
XLA Modules:
  0.0 123.3 jit_solution(2839292773511230879)
XLA Ops:
  0.6 0.0 copy-start
  0.6 0.0 copy-start.1
  0.7 1.1 pad_maximum_fusion.xy_ref
  1.7 3.7 %first_rows.1 = (f32[1,2048]{1,0:T(1,128)S(1)}, bf16[112,2048]{1,0:T(8,128)(2,1)S(1)}, bf16[112,2048]{1,0:T(8,128)(2,1)S(1)}, f32[1,2048]{1,0:T(1,128)S(1)}, f32...) custom-call(bf16[64,2048]{1,0:T(8,128)(2,1)S(1)} %pad_maximum_fusion, ...), custom_call_target="tpu_custom_call" | custom-call | flops 4000000000 | bytes 1048576 | tf_op jit(solution)/shard_map/first_rows/pallas_call | solution.py:287
  5.4 0.1 collective-permute-start
  5.5 1.2 collective-permute-done.other
  6.7 22.5 %all_to_all.25.parts = f32[8,1,2048]{2,1,0:T(1,128)S(1)} all-to-all(f32[8,1,2048]{2,1,0:T(1,128)S(1)} %pair.2), channel_id=1, replica_groups={{0,2,4,6,8,10,12,14},{1,3,5,7,9,11,13,15},{16,18,20,22,24,26,28,30},{17..., dimensions={0} | all-to-all | bytes 131072 | tf_op jit(solution)/shard_map/all_to_all | solution.py:248
  29.2 0.0 copy-done
  29.2 0.0 copy-done.1
  29.2 9.3 %columns.1 = (f32[16,1,2048]{2,1,0:T(1,128)S(1)}, bf16[128,2048]{1,0:T(8,128)(2,1)S(1)}) custom-call(f32[8,1,2048]{2,1,0:T(1,128)S(1)} %all_to_all.25.parts, f32[1,2048]{1,0:T(1,128)S(1)} %bitcast.4, bf16[2048,128]{1,0:T(8,128)(2,1)S(1)} %copy-done, f32[1,2048]{1,0:T(1,128)S(1)} %get-tuple-element.18.shift, bf16[2048,2048]{1,0:T(8,128)(2,1)S(1)} %get-tuple-element.19.kernel, ...), custom_call_target="tpu_custom_call" | custom-call | flops 10000000 | bytes 1048576 | tf_op jit(solution)/shard_map/columns/pallas_call | solution.py:298
  38.5 13.6 %all_to_all.26.parts = f32[16,1,2048]{2,1,0:T(1,128)S(1)} all-to-all(f32[16,1,2048]{2,1,0:T(1,128)S(1)} %get-tuple-element.24), channel_id=1, replica_groups={{0,16,32,48,80,96,112,64,160,176,128,144,240,192,208,224},{1,17,33,49,8..., dimensions={0} | all-to-all | bytes 262144 | tf_op jit(solution)/shard_map/all_to_all | solution.py:248
  52.1 1.6 %rows.1.own = f32[1,2048]{1,0:T(1,128)S(1)} custom-call(f32[16,1,2048]{2,1,0:T(1,128)S(1)} %all_to_all.26.parts, f32[1,2048]{1,0:T(1,128)S(1)} %get-tuple-element.18.shift, bf16[2048,2048]{1,0:T(8,128)(2,1)S(1)} %get-tuple-element.25.across, bf16[112,2048]{1,0:T(8,128)(2,1)S(1)} %get-tuple-element.20.left0, bf16[112,2048]{1,0:T(8,128)(2,1)S(1)} %get-tuple-element.21.right0, ...), custom_call_target="tpu_custom_call" | custom-call | flops 10000000 | bytes 1048576 | tf_op jit(solution)/shard_map/rows/pallas_call | solution.py:306
  53.7 0.1 collective-permute-start.1
  53.8 1.2 collective-permute-done.1.other
  55.0 10.8 %all_to_all.27.parts = f32[8,1,2048]{2,1,0:T(1,128)S(1)} all-to-all(f32[8,1,2048]{2,1,0:T(1,128)S(1)} %pair.3), channel_id=1, replica_groups={{0,2,4,6,8,10,12,14},{1,3,5,7,9,11,13,15},{16,18,20,22,24,26,28,30},{17..., dimensions={0} | all-to-all | bytes 131072 | tf_op jit(solution)/shard_map/all_to_all | solution.py:248
  65.7 17.2 %carry.1 = (f32[1,2048]{1,0:T(1,128)}, f32[16,144,128]{2,1,0:T(8,128)S(1)}) custom-call(f32[8,1,2048]{2,1,0:T(1,128)S(1)} %all_to_all.27.parts, f32[1,2048]{1,0:T(1,128)S(1)} %bitcast.5, f32[1,2048]{1,0:T(1,128)S(1)} %get-tuple-element.18.shift, bf16[2048,2048]{1,0:T(8,128)(2,1)S(1)} %get-tuple-element.19.kernel, ...), custom_call_target="tpu_custom_call" | custom-call | flops 10000000 | bytes 1048576 | tf_op jit(solution)/shard_map/carry/pallas_call | solution.py:310
  82.9 20.7 %all_to_all.28.parts = f32[16,144,128]{2,1,0:T(8,128)S(1)} all-to-all(f32[16,144,128]{2,1,0:T(8,128)S(1)} %get-tuple-element.28), channel_id=1, replica_groups={{0,16,32,48,80,96,112,64,160,176,128,144,240,192,208,224},{1,17,33,49,8..., dimensions={0} | all-to-all | bytes 2359296 | tf_op jit(solution)/shard_map/all_to_all | solution.py:248
  103.6 0.8 finish.1
  104.3 18.0 %all_to_all.29 = f32[16,128,128]{2,1,0:T(8,128)S(1)} all-to-all(f32[16,128,128]{2,1,0:T(8,128)S(1)} %get-tuple-element.30), channel_id=1, replica_groups={{0,16,32,48,80,96,112,64,160,176,128,144,240,192,208,224},{1,17,33,49,8..., dimensions={0} | all-to-all | bytes 2097152 | tf_op jit(solution)/shard_map/all_to_all | solution.py:248
  122.3 1.0 copy.8
  (3 shorter events, 0.0 us)
Async XLA Ops:
  0.6 28.6 %copy-start = (bf16[2048,128]{1,0:T(8,128)(2,1)S(1)}, bf16[2048,128]{1,0:T(8,128)(2,1)}, u32[]{:S(2)}) copy-start(bf16[2048,128]{1,0:T(8,128)(2,1)} %scores.1) | copy-start | bytes 1572868
  0.6 28.5 %copy-start.1 = (f32[2048]{0:T(1024)S(1)}, f32[2048]{0:T(1024)}, u32[]{:S(2)}) copy-start(f32[2048]{0:T(1024)} %param.6) | copy-start | bytes 24580
  5.4 1.3 %collective-permute-start = (f32[1,2048]{1,0:T(1,128)S(1)}, f32[1,2048]{1,0:T(1,128)S(1)}, u32[]{:S(2)}, u32[]{:S(2)}) collective-permute-start(f32[1,2048]{1,0:T(1,128)S(1)} %get-tuple-element.17.own), channel_id=1, source_target_pairs={{0,1},{1,0},{2,3},{3,2},{4,5},{5,4},{6,7},{7,6},{8,9},{9,8},{10,11... | collective-permute-start | bytes 24584 | tf_op jit(solution)/shard_map/ppermute | solution.py:252
  53.7 1.3 %collective-permute-start.1 = (f32[1,2048]{1,0:T(1,128)S(1)}, f32[1,2048]{1,0:T(1,128)S(1)}, u32[]{:S(2)}, u32[]{:S(2)}) collective-permute-start(f32[1,2048]{1,0:T(1,128)S(1)} %rows.1.own), channel_id=1, source_target_pairs={{0,1},{1,0},{2,3},{3,2},{4,5},{5,4},{6,7},{7,6},{8,9},{9,8},{10,11... | collective-permute-start | bytes 24584 | tf_op jit(solution)/shard_map/ppermute | solution.py:252
where the time goes:
time: 125 us; the launch traced here: 123 us
  blocking collectives  85.5 us (68%)
  Pallas kernels  32.6 us (26%)
  waiting for transfers between devices  2.32 us (2%)
    all_to_all x5, blocking collectives, exchanged(): return lax.all_to_all(x, axis, 0, 0, tiled=True, axis_index_groups=groups)  85.5 us
    pallas_call x1, Pallas kernels, shards(): call(functools.partial(carry, log_sources), (line, shape((sources, progs...  17.2 us
    pallas_call x1, Pallas kernels, shards(): call(functools.partial(columns, log_sources), (to_sources, shape((progs,...  9.3 us
    pallas_call x1, Pallas kernels, shards(): call(functools.partial(first_rows, scale), (line, operand, operand, line,...  3.68 us
  transfers between devices with their start and end apart: 2, of which 2 were waited for; matrix products, arithmetic and copies ran while one was open for 0% of the time, Pallas kernels for 0%

commit v1 on v0

--- a/solution.py
+++ b/solution.py
@@ -16,7 +16,7 @@
 UNIT = EPSILON * math.log(2.0)
 LOW, HIGH, LEAST = 2.0**-90, 2.0**100, 2.0**-100
 STATIC, DEPTH = 96, 112
-TILE = 256
+TILE, SAMPLE = 256, 64
 f32, bf16 = jnp.float32, jnp.bfloat16
 
 
@@ -100,7 +100,7 @@
     size = xp.shape[1]
     chunk = 512
     for n in range(0, size, chunk):
-        part = jnp.dot(turned[:TILE, :], left[:, n : n + chunk], preferred_element_type=f32)
+        part = jnp.dot(turned[:SAMPLE, :], left[:, n : n + chunk], preferred_element_type=f32)
         shift[:, n : n + chunk] = jnp.max(part, axis=0, keepdims=True)
     set_source(left, -asq[...] - shift[...])
     sums = []
@@ -196,7 +196,7 @@
     low = (scaled - high.astype(f32)).astype(bf16)
     sums = weighted(jnp.concatenate([high, low, rows_of(split3(weight), 16)], axis=0), kernel)
     total = jnp.sum(sums[2 * progs : 2 * progs + 3], axis=0, keepdims=True)
-    put_blocks(out, (sums[:progs] + sums[progs : 2 * progs]) / total, top + jnp.log2(total))
+    put_blocks(out, (sums[:progs] + sums[progs : 2 * progs]) * (1.0 / total), top + jnp.log2(total))
 
     @pl.when(jnp.logical_not(in_range(total, weight)))
     def _():
@@ -252,7 +252,7 @@
     other = lax.ppermute(line, "tgt", [(k, k ^ 1) for k in range(targets)])
     copies = jax.ShapeDtypeStruct((targets // 2, *line.shape), f32)
     merged_line = call(pair, copies, [VMEM] * 2, name="pair")(line, other)
-    chips = [[2 * z + core for z in range(targets // 2)] for core in range(2)]
+    chips = [[2 * ((z // 2 if z % 2 == 0 else targets // 2 - 1 - z // 2)) + core for z in range(targets // 2)] for core in range(2)]
     return exchanged(merged_line, "tgt", chips)
 
 

time: 125 us -> 131 us (1.048); the launches traced: 123 us -> 131 us
  blocking collectives: 85.5 us -> 93.5 us
    all_to_all x5, blocking collectives: 85.5 us -> 93.5 us  [exchanged(): return lax.all_to_all(x, axis, 0, 0, tiled=True, axis_index_groups=groups)]
where the time goes in v1:
time: 131 us
  blocking collectives  93.5 us (71%)
  Pallas kernels  32.6 us (25%)
  waiting for transfers between devices  2.32 us (2%)
    all_to_all x5, blocking collectives, exchanged(): return lax.all_to_all(x, axis, 0, 0, tiled=True, axis_index_groups=groups)  93.5 us
    pallas_call x1, Pallas kernels, shards(): call(functools.partial(carry, log_sources), (line, shape((sources, progs...  17.2 us
    pallas_call x1, Pallas kernels, shards(): call(functools.partial(columns, log_sources), (to_sources, shape((progs,...  9.3 us
    pallas_call x1, Pallas kernels, shards(): call(functools.partial(first_rows, scale), (line, operand, operand, line,...  3.69 us
  transfers between devices with their start and end apart: 2, of which 2 were waited for; matrix products, arithmetic and copies ran while one was open for 0% of the time, Pallas kernels for 0%

profile of v1, /device:TPU:8, one launch (start us, length us, event | category | flops | bytes accessed | tf_op | source)
XLA Modules:
  0.0 131.4 jit_solution(16485912000448838317)
XLA Ops:
  0.6 0.0 copy-start
  0.6 0.0 copy-start.1
  0.7 1.1 pad_maximum_fusion.xy_ref
  1.7 3.7 %first_rows.1 = (f32[1,2048]{1,0:T(1,128)S(1)}, bf16[112,2048]{1,0:T(8,128)(2,1)S(1)}, bf16[112,2048]{1,0:T(8,128)(2,1)S(1)}, f32[1,2048]{1,0:T(1,128)S(1)}, f32...) custom-call(bf16[64,2048]{1,0:T(8,128)(2,1)S(1)} %pad_maximum_fusion, ...), custom_call_target="tpu_custom_call" | custom-call | flops 4000000000 | bytes 1048576 | tf_op jit(solution)/shard_map/first_rows/pallas_call | solution.py:287
  5.4 0.1 collective-permute-start
  5.5 1.2 collective-permute-done.other
  6.7 23.8 %all_to_all.25.parts = f32[8,1,2048]{2,1,0:T(1,128)S(1)} all-to-all(f32[8,1,2048]{2,1,0:T(1,128)S(1)} %pair.2), channel_id=1, replica_groups={{0,14,2,12,4,10,6,8},{1,15,3,13,5,11,7,9},{16,30,18,28,20,26,22,24},{17..., dimensions={0} | all-to-all | bytes 131072 | tf_op jit(solution)/shard_map/all_to_all | solution.py:248
  30.5 0.0 copy-done
  30.5 0.0 copy-done.1
  30.5 9.3 %columns.1 = (f32[16,1,2048]{2,1,0:T(1,128)S(1)}, bf16[128,2048]{1,0:T(8,128)(2,1)S(1)}) custom-call(f32[8,1,2048]{2,1,0:T(1,128)S(1)} %all_to_all.25.parts, f32[1,2048]{1,0:T(1,128)S(1)} %bitcast.4, bf16[2048,128]{1,0:T(8,128)(2,1)S(1)} %copy-done, f32[1,2048]{1,0:T(1,128)S(1)} %get-tuple-element.18.shift, bf16[2048,2048]{1,0:T(8,128)(2,1)S(1)} %get-tuple-element.19.kernel, ...), custom_call_target="tpu_custom_call" | custom-call | flops 10000000 | bytes 1048576 | tf_op jit(solution)/shard_map/columns/pallas_call | solution.py:298
  39.8 13.6 %all_to_all.26.parts = f32[16,1,2048]{2,1,0:T(1,128)S(1)} all-to-all(f32[16,1,2048]{2,1,0:T(1,128)S(1)} %get-tuple-element.24), channel_id=1, replica_groups={{0,16,32,48,80,96,112,64,160,176,128,144,240,192,208,224},{1,17,33,49,8..., dimensions={0} | all-to-all | bytes 262144 | tf_op jit(solution)/shard_map/all_to_all | solution.py:248
  53.4 1.6 %rows.1.own = f32[1,2048]{1,0:T(1,128)S(1)} custom-call(f32[16,1,2048]{2,1,0:T(1,128)S(1)} %all_to_all.26.parts, f32[1,2048]{1,0:T(1,128)S(1)} %get-tuple-element.18.shift, bf16[2048,2048]{1,0:T(8,128)(2,1)S(1)} %get-tuple-element.25.across, bf16[112,2048]{1,0:T(8,128)(2,1)S(1)} %get-tuple-element.20.left0, bf16[112,2048]{1,0:T(8,128)(2,1)S(1)} %get-tuple-element.21.right0, ...), custom_call_target="tpu_custom_call" | custom-call | flops 10000000 | bytes 1048576 | tf_op jit(solution)/shard_map/rows/pallas_call | solution.py:306
  55.0 0.1 collective-permute-start.1
  55.1 1.2 collective-permute-done.1.other
  56.3 15.2 %all_to_all.27.parts = f32[8,1,2048]{2,1,0:T(1,128)S(1)} all-to-all(f32[8,1,2048]{2,1,0:T(1,128)S(1)} %pair.3), channel_id=1, replica_groups={{0,14,2,12,4,10,6,8},{1,15,3,13,5,11,7,9},{16,30,18,28,20,26,22,24},{17..., dimensions={0} | all-to-all | bytes 131072 | tf_op jit(solution)/shard_map/all_to_all | solution.py:248
  71.5 17.2 %carry.1 = (f32[1,2048]{1,0:T(1,128)}, f32[16,144,128]{2,1,0:T(8,128)S(1)}) custom-call(f32[8,1,2048]{2,1,0:T(1,128)S(1)} %all_to_all.27.parts, f32[1,2048]{1,0:T(1,128)S(1)} %bitcast.5, f32[1,2048]{1,0:T(1,128)S(1)} %get-tuple-element.18.shift, bf16[2048,2048]{1,0:T(8,128)(2,1)S(1)} %get-tuple-element.19.kernel, ...), custom_call_target="tpu_custom_call" | custom-call | flops 10000000 | bytes 1048576 | tf_op jit(solution)/shard_map/carry/pallas_call | solution.py:310
  88.6 22.9 %all_to_all.28.parts = f32[16,144,128]{2,1,0:T(8,128)S(1)} all-to-all(f32[16,144,128]{2,1,0:T(8,128)S(1)} %get-tuple-element.28), channel_id=1, replica_groups={{0,16,32,48,80,96,112,64,160,176,128,144,240,192,208,224},{1,17,33,49,8..., dimensions={0} | all-to-all | bytes 2359296 | tf_op jit(solution)/shard_map/all_to_all | solution.py:248
  111.6 0.8 finish.1
  112.3 18.1 %all_to_all.29 = f32[16,128,128]{2,1,0:T(8,128)S(1)} all-to-all(f32[16,128,128]{2,1,0:T(8,128)S(1)} %get-tuple-element.30), channel_id=1, replica_groups={{0,16,32,48,80,96,112,64,160,176,128,144,240,192,208,224},{1,17,33,49,8..., dimensions={0} | all-to-all | bytes 2097152 | tf_op jit(solution)/shard_map/all_to_all | solution.py:248
  130.4 1.0 copy.8
  (3 shorter events, 0.0 us)
Async XLA Ops:
  0.6 29.9 %copy-start = (bf16[2048,128]{1,0:T(8,128)(2,1)S(1)}, bf16[2048,128]{1,0:T(8,128)(2,1)}, u32[]{:S(2)}) copy-start(bf16[2048,128]{1,0:T(8,128)(2,1)} %scores.1) | copy-start | bytes 1572868
  0.6 29.9 %copy-start.1 = (f32[2048]{0:T(1024)S(1)}, f32[2048]{0:T(1024)}, u32[]{:S(2)}) copy-start(f32[2048]{0:T(1024)} %param.6) | copy-start | bytes 24580
  5.4 1.3 collective-permute-start
  55.0 1.3 collective-permute-start.1

commit v2 on v1

--- a/solution.py
+++ b/solution.py
@@ -104,15 +104,16 @@
         shift[:, n : n + chunk] = jnp.max(part, axis=0, keepdims=True)
     set_source(left, -asq[...] - shift[...])
     sums = []
+    chunk, tile = 256, 512
     for n in range(0, size, chunk):
         total = jnp.zeros((8, chunk), f32)
-        for k in range(0, size, TILE):
-            part = jnp.dot(turned[k : k + TILE, :], left[:, n : n + chunk], preferred_element_type=f32)
+        for k in range(0, size, tile):
+            part = jnp.dot(turned[k : k + tile, :], left[:, n : n + chunk], preferred_element_type=f32)
             part = jnp.exp2(part)
             low = part.astype(bf16)
-            across[k : k + TILE, n : n + chunk] = low
-            kernel[n : n + chunk, k : k + TILE] = jnp.transpose(low)
-            total = total + jnp.sum(part.reshape(TILE // 8, 8, chunk), axis=0)
+            across[k : k + tile, n : n + chunk] = low
+            kernel[n : n + chunk, k : k + tile] = jnp.transpose(low)
+            total = total + jnp.sum(part.reshape(tile // 8, 8, chunk), axis=0)
         sums.append(jnp.sum(total, axis=0, keepdims=True))
     total = jnp.concatenate(sums, axis=1)
     out[...] = shift[...] + jnp.log2(total)

time: 131 us -> 126 us (0.962); the launches traced: 131 us -> 124 us
  blocking collectives: 93.5 us -> 86.7 us
    all_to_all x5, blocking collectives: 93.5 us -> 86.7 us  [exchanged(): return lax.all_to_all(x, axis, 0, 0, tiled=True, axis_index_groups=groups)]
where the time goes in v2:
time: 126 us; the launch traced here: 124 us
  blocking collectives  86.7 us (69%)
  Pallas kernels  32.4 us (26%)
  waiting for transfers between devices  2.32 us (2%)
    all_to_all x5, blocking collectives, exchanged(): return lax.all_to_all(x, axis, 0, 0, tiled=True, axis_index_groups=groups)  86.7 us
    pallas_call x1, Pallas kernels, shards(): call(functools.partial(carry, log_sources), (line, shape((sources, progs...  17.2 us
    pallas_call x1, Pallas kernels, shards(): call(functools.partial(columns, log_sources), (to_sources, shape((progs,...  9.3 us
    pallas_call x1, Pallas kernels, shards(): call(functools.partial(first_rows, scale), (line, operand, operand, line,...  3.54 us
  transfers between devices with their start and end apart: 2, of which 2 were waited for; matrix products, arithmetic and copies ran while one was open for 0% of the time, Pallas kernels for 0%

profile of v2, /device:TPU:8, one launch (start us, length us, event | category | flops | bytes accessed | tf_op | source)
XLA Modules:
  0.0 124.3 jit_solution(11679241476119709531)
XLA Ops:
  0.6 0.0 copy-start
  0.6 0.0 copy-start.1
  0.7 1.1 pad_maximum_fusion.xy_ref
  1.7 3.5 %first_rows.1 = (f32[1,2048]{1,0:T(1,128)S(1)}, bf16[112,2048]{1,0:T(8,128)(2,1)S(1)}, bf16[112,2048]{1,0:T(8,128)(2,1)S(1)}, f32[1,2048]{1,0:T(1,128)S(1)}, f32...) custom-call(bf16[64,2048]{1,0:T(8,128)(2,1)S(1)} %pad_maximum_fusion, ...), custom_call_target="tpu_custom_call" | custom-call | flops 4000000000 | bytes 1048576 | tf_op jit(solution)/shard_map/first_rows/pallas_call | solution.py:288
  5.3 0.1 collective-permute-start
  5.4 1.2 collective-permute-done.other
  6.6 22.9 %all_to_all.25.parts = f32[8,1,2048]{2,1,0:T(1,128)S(1)} all-to-all(f32[8,1,2048]{2,1,0:T(1,128)S(1)} %pair.2), channel_id=1, replica_groups={{0,14,2,12,4,10,6,8},{1,15,3,13,5,11,7,9},{16,30,18,28,20,26,22,24},{17..., dimensions={0} | all-to-all | bytes 131072 | tf_op jit(solution)/shard_map/all_to_all | solution.py:249
  29.4 0.0 copy-done
  29.4 0.0 copy-done.1
  29.4 9.3 %columns.1 = (f32[16,1,2048]{2,1,0:T(1,128)S(1)}, bf16[128,2048]{1,0:T(8,128)(2,1)S(1)}) custom-call(f32[8,1,2048]{2,1,0:T(1,128)S(1)} %all_to_all.25.parts, f32[1,2048]{1,0:T(1,128)S(1)} %bitcast.4, bf16[2048,128]{1,0:T(8,128)(2,1)S(1)} %copy-done, f32[1,2048]{1,0:T(1,128)S(1)} %get-tuple-element.18.shift, bf16[2048,2048]{1,0:T(8,128)(2,1)S(1)} %get-tuple-element.19.kernel, ...), custom_call_target="tpu_custom_call" | custom-call | flops 10000000 | bytes 1048576 | tf_op jit(solution)/shard_map/columns/pallas_call | solution.py:299
  38.8 14.4 %all_to_all.26.parts = f32[16,1,2048]{2,1,0:T(1,128)S(1)} all-to-all(f32[16,1,2048]{2,1,0:T(1,128)S(1)} %get-tuple-element.24), channel_id=1, replica_groups={{0,16,32,48,80,96,112,64,160,176,128,144,240,192,208,224},{1,17,33,49,8..., dimensions={0} | all-to-all | bytes 262144 | tf_op jit(solution)/shard_map/all_to_all | solution.py:249
  53.2 1.6 %rows.1.own = f32[1,2048]{1,0:T(1,128)S(1)} custom-call(f32[16,1,2048]{2,1,0:T(1,128)S(1)} %all_to_all.26.parts, f32[1,2048]{1,0:T(1,128)S(1)} %get-tuple-element.18.shift, bf16[2048,2048]{1,0:T(8,128)(2,1)S(1)} %get-tuple-element.25.across, bf16[112,2048]{1,0:T(8,128)(2,1)S(1)} %get-tuple-element.20.left0, bf16[112,2048]{1,0:T(8,128)(2,1)S(1)} %get-tuple-element.21.right0, ...), custom_call_target="tpu_custom_call" | custom-call | flops 10000000 | bytes 1048576 | tf_op jit(solution)/shard_map/rows/pallas_call | solution.py:307
  54.8 0.1 collective-permute-start.1
  54.9 1.2 collective-permute-done.1.other
  56.1 10.7 %all_to_all.27.parts = f32[8,1,2048]{2,1,0:T(1,128)S(1)} all-to-all(f32[8,1,2048]{2,1,0:T(1,128)S(1)} %pair.3), channel_id=1, replica_groups={{0,14,2,12,4,10,6,8},{1,15,3,13,5,11,7,9},{16,30,18,28,20,26,22,24},{17..., dimensions={0} | all-to-all | bytes 131072 | tf_op jit(solution)/shard_map/all_to_all | solution.py:249
  66.7 17.2 %carry.1 = (f32[1,2048]{1,0:T(1,128)}, f32[16,144,128]{2,1,0:T(8,128)S(1)}) custom-call(f32[8,1,2048]{2,1,0:T(1,128)S(1)} %all_to_all.27.parts, f32[1,2048]{1,0:T(1,128)S(1)} %bitcast.5, f32[1,2048]{1,0:T(1,128)S(1)} %get-tuple-element.18.shift, bf16[2048,2048]{1,0:T(8,128)(2,1)S(1)} %get-tuple-element.19.kernel, ...), custom_call_target="tpu_custom_call" | custom-call | flops 10000000 | bytes 1048576 | tf_op jit(solution)/shard_map/carry/pallas_call | solution.py:311
  83.9 20.7 %all_to_all.28.parts = f32[16,144,128]{2,1,0:T(8,128)S(1)} all-to-all(f32[16,144,128]{2,1,0:T(8,128)S(1)} %get-tuple-element.28), channel_id=1, replica_groups={{0,16,32,48,80,96,112,64,160,176,128,144,240,192,208,224},{1,17,33,49,8..., dimensions={0} | all-to-all | bytes 2359296 | tf_op jit(solution)/shard_map/all_to_all | solution.py:249
  104.6 0.8 finish.1
  105.3 18.0 %all_to_all.29 = f32[16,128,128]{2,1,0:T(8,128)S(1)} all-to-all(f32[16,128,128]{2,1,0:T(8,128)S(1)} %get-tuple-element.30), channel_id=1, replica_groups={{0,16,32,48,80,96,112,64,160,176,128,144,240,192,208,224},{1,17,33,49,8..., dimensions={0} | all-to-all | bytes 2097152 | tf_op jit(solution)/shard_map/all_to_all | solution.py:249
  123.4 1.0 copy.8
  (3 shorter events, 0.0 us)
Async XLA Ops:
  0.6 28.8 %copy-start = (bf16[2048,128]{1,0:T(8,128)(2,1)S(1)}, bf16[2048,128]{1,0:T(8,128)(2,1)}, u32[]{:S(2)}) copy-start(bf16[2048,128]{1,0:T(8,128)(2,1)} %scores.1) | copy-start | bytes 1572868
  0.6 28.8 %copy-start.1 = (f32[2048]{0:T(1024)S(1)}, f32[2048]{0:T(1024)}, u32[]{:S(2)}) copy-start(f32[2048]{0:T(1024)} %param.6) | copy-start | bytes 24580
  5.3 1.3 %collective-permute-start = (f32[1,2048]{1,0:T(1,128)S(1)}, f32[1,2048]{1,0:T(1,128)S(1)}, u32[]{:S(2)}, u32[]{:S(2)}) collective-permute-start(f32[1,2048]{1,0:T(1,128)S(1)} %get-tuple-element.17.own), channel_id=1, source_target_pairs={{0,1},{1,0},{2,3},{3,2},{4,5},{5,4},{6,7},{7,6},{8,9},{9,8},{10,11... | collective-permute-start | bytes 24584 | tf_op jit(solution)/shard_map/ppermute | solution.py:253
  54.8 1.3 %collective-permute-start.1 = (f32[1,2048]{1,0:T(1,128)S(1)}, f32[1,2048]{1,0:T(1,128)S(1)}, u32[]{:S(2)}, u32[]{:S(2)}) collective-permute-start(f32[1,2048]{1,0:T(1,128)S(1)} %rows.1.own), channel_id=1, source_target_pairs={{0,1},{1,0},{2,3},{3,2},{4,5},{5,4},{6,7},{7,6},{8,9},{9,8},{10,11... | collective-permute-start | bytes 24584 | tf_op jit(solution)/shard_map/ppermute | solution.py:253
